TPU v7x, 32 devices: a whole 2x2x4 slice. The times are simulated.
32 devices in a mesh: section: 4 (over z), tensor: 8 (over y, x, core).
Axes of the slice: x: 2, y: 2, z: 4, core: 2. Of those that a mesh axis runs over, the one named last changes fastest.
Arguments:
- hidden: bfloat16 [32, 8192], P('section', 'tensor'), may hold values from -33 to 33, as said below
- out_weight: bfloat16 [4096, 8192], P(('section', 'tensor')), may hold values from -12 to 12, as said below
- targets: int32 [32], replicated, may hold values from 0 to 4095
- token_mask: int32 [32], replicated, may hold values 0 or 1
Outputs:
- ce_loss: float32 [], replicated
- z_loss: float32 [], replicated
- grad_hidden: float32 [32, 8192], P('section', 'tensor')
- grad_weight: bfloat16 [4096, 8192], P(('section', 'tensor'))
Inputs may be any that keep to these rules, and one draw needn't show every extreme that they name: hidden rows of one token have one scale; entries are bounded. `out_weight`: entries are bounded.
All inputs are finite; a program needn't handle non-finite values.
Results may differ from a plain program's by a relative error of at most 0.0026.
Values may be sent and summed in bfloat16 or wider, within the bound.
No kernel may reach another device: no remote copies, remote signals or barrier semaphores. Data moves between devices by JAX's collectives and lax.ppermute only.
A program may use at most 64 MiB of HBM per device.

v0:
```python
import jax
import jax.numpy as jnp
from jax import lax
from jax.sharding import PartitionSpec as P

z_weight = 0.0001


def body(hidden, out_weight, targets, token_mask):
    vocab_dev = out_weight.shape[0]
    full_rows = lax.all_gather(hidden, "tensor", axis=1, tiled=True)
    gathered = lax.all_gather(full_rows, "section", axis=0, tiled=True)
    token_count = gathered.shape[0]
    logits = lax.dot_general(
        gathered, out_weight, (((1,), (1,)), ((), ())), preferred_element_type=jnp.float32
    )
    vocab_start = (
        lax.axis_index("section") * lax.axis_size("tensor") + lax.axis_index("tensor")
    ) * vocab_dev
    local_ids = targets - vocab_start
    target_hit = local_ids[:, None] == jnp.arange(vocab_dev, dtype=jnp.int32)[None, :]
    picked_local = jnp.sum(jnp.where(target_hit, logits, 0.0), axis=1)
    local_top = jnp.max(logits, axis=1)
    row_top = lax.pmax(local_top, ("section", "tensor"))
    local_total = jnp.sum(jnp.exp(logits - row_top[:, None]), axis=1)
    row_total, picked = lax.psum((local_total, picked_local), ("section", "tensor"))
    log_total = row_top + jnp.log(row_total)
    kept = token_mask.astype(jnp.float32)
    ce_loss = jnp.sum(kept * (log_total - picked)) / token_count
    z_loss = jnp.sum(kept * log_total * log_total) / token_count
    factor = 1.0 + 2.0 * z_weight * log_total
    probs = jnp.exp(logits - log_total[:, None])
    dlogits = (kept[:, None] * (factor[:, None] * probs - target_hit.astype(jnp.float32))).astype(
        jnp.bfloat16
    )
    grad_weight = lax.dot_general(
        dlogits, gathered, (((0,), (0,)), ((), ())), preferred_element_type=jnp.float32
    ).astype(jnp.bfloat16)
    width_part = lax.psum_scatter(
        lax.dot_general(
            out_weight, dlogits, (((0,), (1,)), ((), ())), preferred_element_type=jnp.float32
        ),
        "tensor",
        scatter_dimension=0,
        tiled=True,
    )
    mine = lax.psum_scatter(width_part, "section", scatter_dimension=1, tiled=True)
    grad_hidden = mine.T
    return (ce_loss, z_loss, grad_hidden, grad_weight)


def solution(mesh):
    placed = (P("section", "tensor"), P(("section", "tensor"), None), P(), P())
    return jax.shard_map(
        body,
        mesh=mesh,
        in_specs=placed,
        out_specs=(P(), P(), P("section", "tensor"), P(("section", "tensor"), None)),
        check_vma=False,
    )
```

profile of v0, /device:TPU:0, one launch (start us, length us, event | category | flops | bytes accessed | tf_op | source)
XLA Modules:
  0.0 185.8 jit_solution(5926214995159261907)
XLA Ops:
  7.2 0.0 copy-start
  7.2 0.0 copy-start.2
  7.2 0.0 reduce-scatter.3.cloned.1.call-start
  7.2 0.8 convert_element_type.12
  8.0 10.9 %all_gather.6 = bf16[8,8192]{1,0:T(8,128)(2,1)S(1)} all-gather(bf16[8,1024]{1,0:T(8,128)(2,1)} %param.4), channel_id=1, replica_groups=mesh['section'=4,'tensor'=8] {'tensor'}, dimensions={1}, use_global_device_ids=true | all-gather | bytes 147456 | tf_op jit(solution)/shard_map/all_gather | solution.py:11
  18.9 16.3 %all_gather.7 = bf16[32,8192]{1,0:T(8,128)(2,1)S(1)} all-gather(bf16[8,8192]{1,0:T(8,128)(2,1)S(1)} %all_gather.6), channel_id=1, replica_groups=mesh['section'=4,'tensor'=8] {'section'}, dimensions={0}, use_global_device_ids=true | all-gather | bytes 655360 | tf_op jit(solution)/shard_map/all_gather | solution.py:12
  35.2 0.0 copy-done
  35.2 0.9 fusion.1
  36.1 39.6 %pmax.7 = f32[32]{0:T(128)S(1)} all-reduce(f32[32]{0:T(128)S(1)} %get-tuple-element.12), channel_id=1, replica_groups=mesh['section'=4,'tensor'=8] {'section','tensor'}, use_global_device_ids=true, to_apply=%region_1.2 | all-reduce | flops 32 | bytes 256 | tf_op jit(solution)/shard_map/pmax | solution.py:24
  75.7 0.0 copy-done.2
  75.7 0.2 select_reduce_fusion
  75.9 41.0 %all-reduce = (f32[32]{0:T(128)S(1)}, f32[32]{0:T(128)S(1)}) all-reduce(f32[32]{0:T(128)S(1)} %get-tuple-element.5, f32[32]{0:T(128)S(1)} %get-tuple-element.4), channel_id=1, replica_groups=mesh['section'=4,'tensor'=8] {'section','tensor'}, use_global_device_ids=true, to_apply=%region_3.4 | all-reduce | flops 64 | bytes 512 | tf_op jit(solution)/shard_map/psum | solution.py:26
  116.9 0.0 copy-start.1
  116.9 1.4 convolution_bitcast_fusion
  118.3 0.0 reduce-scatter.3.cloned.1.call-update
  118.4 0.0 reduce-scatter.5.cloned.1.call-start
  118.4 0.0 copy-done.1
  118.4 0.6 fusion
  120.3 34.1 %reduce-scatter.3.cloned.1.call-done = f32[1024,32]{0,1:T(8,128)} async-done(((f32[8192,32]{0,1:T(8,128)}), f32[1024,32]{0,1:T(8,128)}) %reduce-scatter.3.cloned.1.call-update) | async-done | bytes 131088 | tf_op jit(solution)/shard_map/reduce_scatter | solution.py:39
  154.4 0.0 reduce-scatter.5.cloned.1.call-update
  154.4 2.1 %convolution_convert_fusion = bf16[128,8192]{1,0:T(8,128)(2,1)} fusion(bf16[32,8192]{1,0:T(8,128)(2,1)S(1)} %all_gather.7, f32[32,128]{1,0:T(8,128)S(1)} %get-tuple-element.13, f32[32]{0:T(128)S(1)} %get-tuple-element.11, f32[32]{0:T(128)S(1)} %get-tuple-element.10, f32[32]{0:T(128)S(1)} %convert_element_type.12, s32[32]{0:T(128)S(1)} %broadcast_subtract_fusion), kind=kOutput, calls=%fused_computation | convolution fusion | flops 68186112 | bytes 2638336 | tf_op jit(solution)/shard_map/dot_general | solution.py:36
  156.6 20.1 %reduce-scatter.5.cloned.1.call-done = f32[1024,8]{0,1:T(8,128)} async-done(((f32[1024,32]{0,1:T(8,128)}), f32[1024,8]{0,1:T(8,128)}) %reduce-scatter.5.cloned.1.call-update) | async-done | bytes 32784 | tf_op jit(solution)/shard_map/reduce_scatter | solution.py:47
  (2 shorter events, 0.0 us)
Async XLA Ops:
  7.2 28.1 %copy-start = (bf16[128,8192]{1,0:T(8,128)(2,1)S(1)}, bf16[128,8192]{1,0:T(8,128)(2,1)}, u32[]{:S(2)}) copy-start(bf16[128,8192]{1,0:T(8,128)(2,1)} %param.5) | copy-start | bytes 6291460
  7.2 68.5 %copy-start.2 = (s32[32]{0:T(128)S(1)}, s32[32]{0:T(128)}, u32[]{:S(2)}) copy-start(s32[32]{0:T(128)} %param.6) | copy-start | bytes 388
  7.2 147.2 %reduce-scatter.3.cloned.1.call-start = ((), (), s32[]{:S(2)}) async-start(), calls=%async_computation.2 | async-start | bytes 1179648 | tf_op jit(solution)/shard_map/reduce_scatter | solution.py:39
  116.9 1.5 copy-start.1
  118.4 58.3 %reduce-scatter.5.cloned.1.call-start = ((), (), s32[]{:S(2)}) async-start(), calls=%async_computation.3 | async-start | bytes 163840 | tf_op jit(solution)/shard_map/reduce_scatter | solution.py:47
Sparse Core Ops, SparseCore 0:
  118.5 35.8 reduce-scatter.2
  157.2 19.4 reduce-scatter.4
where the time goes:
time: 186 us
  blocking collectives  108 us (58%)
  waiting for transfers between devices  54.2 us (29%)
  between operations  17.6 us (9%)
  matrix products  4.48 us (2%)
    psum x1, blocking collectives, body(): lax.psum((local_total, picked_local), ('section', 'tensor'))  41 us
    pmax x1, blocking collectives, body(): row_top = lax.pmax(local_top, ('section', 'tensor'))  39.6 us
    reduce_scatter x1, waiting for transfers between devices, body(): lax.psum_scatter(lax.dot_general(out_weight, dlogits, (((0,), (1,)), ((),...  34.1 us
    reduce_scatter x1, waiting for transfers between devices, body(): lax.psum_scatter(width_part, 'section', scatter_dimension=1, tiled=True)  20.1 us
    all_gather x1, blocking collectives, body(): gathered = lax.all_gather(full_rows, 'section', axis=0, tiled=True)  16.3 us
    all_gather x1, blocking collectives, body(): full_rows = lax.all_gather(hidden, 'tensor', axis=1, tiled=True)  10.9 us
  transfers between devices with their start and end apart: 2, of which 2 were waited for; matrix products, arithmetic and copies ran while one was open for 1% of the time, Pallas kernels for 0%

commit v1 on v0

--- a/solution.py
+++ b/solution.py
@@ -7,6 +7,12 @@
 
 
 def body(hidden, out_weight, targets, token_mask):
+
+    def carry_inputs_now(device_axis, field, across):
+        response = lax.psum(field, axis_name=across)
+        part_next = lax.psum(response, axis_name=device_axis)
+        return part_next
+
     vocab_dev = out_weight.shape[0]
     full_rows = lax.all_gather(hidden, "tensor", axis=1, tiled=True)
     gathered = lax.all_gather(full_rows, "section", axis=0, tiled=True)
@@ -23,7 +29,7 @@
     local_top = jnp.max(logits, axis=1)
     row_top = lax.pmax(local_top, ("section", "tensor"))
     local_total = jnp.sum(jnp.exp(logits - row_top[:, None]), axis=1)
-    row_total, picked = lax.psum((local_total, picked_local), ("section", "tensor"))
+    row_total, picked = carry_inputs_now("section", (local_total, picked_local), "tensor")
     log_total = row_top + jnp.log(row_total)
     kept = token_mask.astype(jnp.float32)
     ce_loss = jnp.sum(kept * (log_total - picked)) / token_count

time: 186 us -> 165 us (0.89)
  blocking collectives: 108 us -> 89.5 us
  waiting for transfers between devices: 54.2 us -> 51.5 us
    psum x1 -> x2, blocking collectives: 41 us -> 22.8 us  [the longest x1 12.7 us: carry_inputs_now(): response = lax.psum(field, axis_name=across)]
    reduce_scatter x1, waiting for transfers between devices: 34.1 us -> 31.3 us  [body(): lax.psum_scatter(lax.dot_general(out_weight, dlogits, (((0,), (1,)), ((),...]
  transfers between devices with their start and end apart: 2 -> 2, of which waited for: 2 -> 2; matrix products, arithmetic and copies ran while one was open for 1% -> 2% of each run, Pallas kernels for 0% -> 0%
where the time goes in v1:
time: 165 us
  blocking collectives  89.5 us (54%)
  waiting for transfers between devices  51.5 us (31%)
  between operations  17.6 us (11%)
  matrix products  4.49 us (3%)
    pmax x1, blocking collectives, body(): row_top = lax.pmax(local_top, ('section', 'tensor'))  39.6 us
    reduce_scatter x1, waiting for transfers between devices, body(): lax.psum_scatter(lax.dot_general(out_weight, dlogits, (((0,), (1,)), ((),...  31.3 us
    reduce_scatter x1, waiting for transfers between devices, body(): lax.psum_scatter(width_part, 'section', scatter_dimension=1, tiled=True)  20.1 us
    all_gather x1, blocking collectives, body(): gathered = lax.all_gather(full_rows, 'section', axis=0, tiled=True)  16.3 us
    psum x1, blocking collectives, carry_inputs_now(): response = lax.psum(field, axis_name=across)  12.7 us
    all_gather x1, blocking collectives, body(): full_rows = lax.all_gather(hidden, 'tensor', axis=1, tiled=True)  10.9 us
    psum x1, blocking collectives, carry_inputs_now(): part_next = lax.psum(response, axis_name=device_axis)  10.1 us
  transfers between devices with their start and end apart: 2, of which 2 were waited for; matrix products, arithmetic and copies ran while one was open for 2% of the time, Pallas kernels for 0%

profile of v1, /device:TPU:0, one launch (start us, length us, event | category | flops | bytes accessed | tf_op | source)
XLA Modules:
  0.0 164.8 jit_solution(9147936822885530075)
XLA Ops:
  7.2 0.0 copy-start
  7.2 0.0 copy-start.2
  7.2 0.0 reduce-scatter.3.cloned.1.call-start
  7.2 0.8 convert_element_type.12
  8.0 10.9 %all_gather.6 = bf16[8,8192]{1,0:T(8,128)(2,1)S(1)} all-gather(bf16[8,1024]{1,0:T(8,128)(2,1)} %param.4), channel_id=1, replica_groups=mesh['section'=4,'tensor'=8] {'tensor'}, dimensions={1}, use_global_device_ids=true | all-gather | bytes 147456 | tf_op jit(solution)/shard_map/all_gather | solution.py:17
  18.9 16.3 %all_gather.7 = bf16[32,8192]{1,0:T(8,128)(2,1)S(1)} all-gather(bf16[8,8192]{1,0:T(8,128)(2,1)S(1)} %all_gather.6), channel_id=1, replica_groups=mesh['section'=4,'tensor'=8] {'section'}, dimensions={0}, use_global_device_ids=true | all-gather | bytes 655360 | tf_op jit(solution)/shard_map/all_gather | solution.py:18
  35.2 0.0 copy-done
  35.2 0.9 fusion.1
  36.1 39.6 %pmax.7 = f32[32]{0:T(128)S(1)} all-reduce(f32[32]{0:T(128)S(1)} %get-tuple-element.14), channel_id=1, replica_groups=mesh['section'=4,'tensor'=8] {'section','tensor'}, use_global_device_ids=true, to_apply=%region_1.2 | all-reduce | flops 32 | bytes 256 | tf_op jit(solution)/shard_map/pmax | solution.py:30
  75.7 0.0 copy-done.2
  75.7 0.2 select_reduce_fusion
  75.9 12.7 %all-reduce = (f32[32]{0:T(128)S(1)}, f32[32]{0:T(128)S(1)}) all-reduce(f32[32]{0:T(128)S(1)} %get-tuple-element.5, f32[32]{0:T(128)S(1)} %get-tuple-element.4), channel_id=1, replica_groups=mesh['section'=4,'tensor'=8] {'tensor'}, use_global_device_ids=true, to_apply=%region_3.4 | all-reduce | flops 64 | bytes 512 | tf_op jit(solution)/shard_map/psum | solution.py:12
  88.6 10.1 %all-reduce.1 = (f32[32]{0:T(128)S(1)}, f32[32]{0:T(128)S(1)}) all-reduce(f32[32]{0:T(128)S(1)} %get-tuple-element.8, f32[32]{0:T(128)S(1)} %get-tuple-element.9), channel_id=1, replica_groups=mesh['section'=4,'tensor'=8] {'section'}, use_global_device_ids=true, to_apply=%region_4.5 | all-reduce | flops 64 | bytes 512 | tf_op jit(solution)/shard_map/psum | solution.py:13
  98.7 0.0 copy-start.1
  98.7 1.4 convolution_bitcast_fusion
  100.1 0.0 reduce-scatter.3.cloned.1.call-update
  100.1 0.0 reduce-scatter.5.cloned.1.call-start
  100.2 0.0 copy-done.1
  100.2 0.6 fusion
  102.1 31.3 %reduce-scatter.3.cloned.1.call-done = f32[1024,32]{0,1:T(8,128)} async-done(((f32[8192,32]{0,1:T(8,128)}), f32[1024,32]{0,1:T(8,128)}) %reduce-scatter.3.cloned.1.call-update) | async-done | bytes 131088 | tf_op jit(solution)/shard_map/reduce_scatter | solution.py:45
  133.4 0.0 reduce-scatter.5.cloned.1.call-update
  133.5 2.1 %convolution_convert_fusion = bf16[128,8192]{1,0:T(8,128)(2,1)} fusion(bf16[32,8192]{1,0:T(8,128)(2,1)S(1)} %all_gather.7, f32[32,128]{1,0:T(8,128)S(1)} %get-tuple-element.15, f32[32]{0:T(128)S(1)} %get-tuple-element.13, f32[32]{0:T(128)S(1)} %get-tuple-element.12, f32[32]{0:T(128)S(1)} %convert_element_type.12, s32[32]{0:T(128)S(1)} %broadcast_subtract_fusion), kind=kOutput, calls=%fused_computation | convolution fusion | flops 68186112 | bytes 2638336 | tf_op jit(solution)/shard_map/dot_general | solution.py:42
  135.6 20.1 %reduce-scatter.5.cloned.1.call-done = f32[1024,8]{0,1:T(8,128)} async-done(((f32[1024,32]{0,1:T(8,128)}), f32[1024,8]{0,1:T(8,128)}) %reduce-scatter.5.cloned.1.call-update) | async-done | bytes 32784 | tf_op jit(solution)/shard_map/reduce_scatter | solution.py:53
  (2 shorter events, 0.0 us)
Async XLA Ops:
  7.2 28.1 %copy-start = (bf16[128,8192]{1,0:T(8,128)(2,1)S(1)}, bf16[128,8192]{1,0:T(8,128)(2,1)}, u32[]{:S(2)}) copy-start(bf16[128,8192]{1,0:T(8,128)(2,1)} %param.5) | copy-start | bytes 6291460
  7.2 68.5 %copy-start.2 = (s32[32]{0:T(128)S(1)}, s32[32]{0:T(128)}, u32[]{:S(2)}) copy-start(s32[32]{0:T(128)} %param.6) | copy-start | bytes 388
  7.2 126.3 %reduce-scatter.3.cloned.1.call-start = ((), (), s32[]{:S(2)}) async-start(), calls=%async_computation.2 | async-start | bytes 1179648 | tf_op jit(solution)/shard_map/reduce_scatter | solution.py:45
  98.7 1.5 copy-start.1
  100.1 55.6 %reduce-scatter.5.cloned.1.call-start = ((), (), s32[]{:S(2)}) async-start(), calls=%async_computation.3 | async-start | bytes 163840 | tf_op jit(solution)/shard_map/reduce_scatter | solution.py:53
Sparse Core Ops, SparseCore 0:
  100.3 33.1 reduce-scatter.2
  136.3 19.4 reduce-scatter.4
